TPU v7x, 32 devices: a whole 2x2x4 slice. The times are simulated.
32 devices in a mesh: row: 4 (over y, core), col: 8 (over z, x).
Axes of the slice: x: 2, y: 2, z: 4, core: 2. Of those that a mesh axis runs over, the one named last changes fastest.
Arguments:
- front: float32 [12288, 12288], P('row', 'col'), may hold values from -6 to 6
- delayed: float32 [64, 12288], P('col', 'row'), may hold values from -6 to 6
- dest: int32 [64], P('col'), may hold values from 0 to 1023, as said below
- pivots: int32 [1024], replicated, may hold values from 0 to 12287, as said below
- pair_flags: int32 [1024], replicated, may hold values from 0 to 1, as said below
- linv: float32 [4, 256, 256], replicated, as said below
- dinv_diag: float32 [1024], replicated, may hold values from -0.1 to 0.1
- dinv_off: float32 [1024], replicated, may hold values from -0.08 to 0.08
Outputs:
- trailing: float32 [12288, 12288], P('row', 'col')
- factor: float32 [12288, 1024], P('row')
Inputs may be any that keep to these rules, and one draw needn't show every extreme that they name: Distinct front columns; slots p * 256 to (p + 1) * 256 - 1 are panel p's pivots. Each block of 1536 columns held by one index of col contains exactly 128 of them. `pair_flags`: A 1 at slot s joins slots s and s + 1 into one 2x2 block; no two 1s are adjacent and the last slot of a panel holds 0. `dest`: several delayed columns may share a slot. Of the 8 delayed columns held by one index of col, at most 2 go to pivot columns held by the same index of col. `linv`: each panel's matrix is unit lower triangular: ones on the diagonal, zeros above it.
All inputs are finite; a program needn't handle non-finite values.
Results may differ from a plain program's by a relative error of at most 0.00015.
Values sent between devices are 32-bit elements; how exact they have to be, the bound alone decides.
A program may use at most 192 MiB of HBM per device.

v0:
```python
import jax
import jax.numpy as jnp
from jax import lax
from jax.sharding import PartitionSpec as P

CAP = 2
precise = lax.Precision.HIGHEST


def broadcast(block, axis, holder):
    block = jnp.where(lax.axis_index(axis) == holder, block, jnp.zeros_like(block))
    return lax.psum(block, axis)


def pair_scale(scaled, pair_bits, diag_part, off_part):
    coupled = pair_bits.astype(jnp.float32) * off_part
    zero_col = jnp.zeros_like(scaled[:, :1])
    shifted_next = jnp.concatenate([scaled[:, 1:], zero_col], axis=1)
    shifted_prev = jnp.concatenate([zero_col, scaled[:, :-1]], axis=1)
    coupled_prev = jnp.concatenate([jnp.zeros_like(coupled[:1]), coupled[:-1]])
    return scaled * diag_part + shifted_next * coupled + shifted_prev * coupled_prev


def select_columns(matrix, wanted, anchor):
    block_width = matrix.shape[1]
    relative = wanted - anchor
    inside = (relative >= 0) & (relative < block_width)
    clipped = jnp.clip(relative, 0, block_width - 1)
    return jnp.where(inside[None, :], jnp.take(matrix, clipped, axis=1), 0.0)


def select_rows(matrix, wanted, anchor):
    block_height = matrix.shape[0]
    relative = wanted - anchor
    inside = (relative >= 0) & (relative < block_height)
    clipped = jnp.clip(relative, 0, block_height - 1)
    return jnp.where(inside[:, None], jnp.take(matrix, clipped, axis=0), 0.0)


def body(front, delayed, dest, pivots, pair_flags, linv, dinv_diag, dinv_off):
    col_count = lax.axis_size("col")
    rows_blk, cols_blk = front.shape
    row_start = lax.axis_index("row") * rows_blk
    col_start = lax.axis_index("col") * cols_blk
    panel_count = linv.shape[0]
    panel_width = linv.shape[1]
    slot_total = pivots.shape[0]
    slot_ids = jnp.arange(slot_total, dtype=jnp.int32)
    owner_ids = jnp.arange(col_count, dtype=jnp.int32)
    slot_hit = dest[:, None] == slot_ids[None, :]
    targets = jnp.sum(jnp.where(slot_hit, pivots[None, :], 0), axis=1)
    owners = targets // cols_blk
    within = targets - owners * cols_blk
    owner_hit = (owners[:, None] == owner_ids[None, :]).astype(jnp.int32)
    earlier = jnp.cumsum(owner_hit, axis=0) - owner_hit
    rank_in = jnp.sum(earlier * owner_hit, axis=1)
    slot_pos = jnp.arange(CAP, dtype=jnp.int32)
    placed = (owner_hit[:, :, None] > 0) & (rank_in[:, None, None] == slot_pos[None, None, :])
    send_vals = jnp.einsum("kos,kr->osr", placed.astype(jnp.float32), delayed, precision=precise)
    send_cols = jnp.sum(jnp.where(placed, within[:, None, None] + 1, 0), axis=0) - 1
    recv_vals, recv_cols = (
        lax.all_to_all(send_vals, "col", split_axis=0, concat_axis=0, tiled=True),
        lax.all_to_all(send_cols, "col", split_axis=0, concat_axis=0, tiled=True),
    )
    flat_vals = recv_vals.reshape(-1, rows_blk)
    flat_cols = recv_cols.reshape(-1)
    col_ids = jnp.arange(cols_blk, dtype=jnp.int32)
    col_hit = (flat_cols[:, None] == col_ids[None, :]).astype(jnp.float32)
    current = front + lax.dot_general(
        flat_vals, col_hit, (((0,), (0,)), ((), ())), precision=precise
    )
    factors = []
    piv_owner = pivots // cols_blk
    piv_hit = (piv_owner[:, None] == owner_ids[None, :]).astype(jnp.int32)
    piv_rank = jnp.sum((jnp.cumsum(piv_hit, axis=0) - piv_hit) * piv_hit, axis=1)
    per_owner = slot_total // col_count
    owned_here = piv_owner == lax.axis_index("col")
    rank_ids = jnp.arange(per_owner, dtype=jnp.int32)
    own_slots = jnp.sum(
        jnp.where(
            owned_here[None, :] & (piv_rank[None, :] == rank_ids[:, None]), slot_ids[None, :], 0
        ),
        axis=1,
    )
    compact = select_columns(current, pivots[own_slots], col_start)
    gathered = lax.all_gather(compact, "col", axis=1, tiled=True)
    every_panel = jnp.take(gathered, piv_owner * per_owner + piv_rank, axis=1)
    previous = []
    for panel_index in range(panel_count):
        offset = panel_index * panel_width
        panel_cols = every_panel[:, offset : offset + panel_width]
        for cols_before, rows_before in previous:
            panel_cols = panel_cols - lax.dot_general(
                cols_before,
                rows_before[offset : offset + panel_width],
                (((1,), (1,)), ((), ())),
                precision=precise,
            )
        finish_offset = panel_index * panel_width
        finish_scaled = jnp.dot(panel_cols, jnp.transpose(linv[panel_index]), precision=precise)
        finish_columns = pair_scale(
            finish_scaled,
            pair_flags[finish_offset : finish_offset + panel_width],
            dinv_diag[finish_offset : finish_offset + panel_width],
            dinv_off[finish_offset : finish_offset + panel_width],
        )
        root_row = col_start // rows_blk
        slice_start = jnp.clip(col_start - row_start, 0, rows_blk - cols_blk)
        root_piece = lax.dynamic_slice_in_dim(finish_scaled, slice_start, cols_blk, 0)
        col_scaled = broadcast(root_piece, "row", root_row)
        current = current - lax.dot_general(
            finish_columns, col_scaled, (((1,), (1,)), ((), ())), precision=precise
        )
        factors.append(finish_columns)
        if panel_index + 1 < panel_count:
            pivot_part = select_rows(finish_scaled, pivots, row_start)
            pivot_rows = lax.psum(pivot_part, "row")
            previous.append((finish_columns, pivot_rows))
    row_ids = row_start + jnp.arange(rows_blk, dtype=jnp.int32)
    row_in = jnp.any(row_ids[:, None] == pivots[None, :], axis=1)
    col_in = jnp.any((col_start + col_ids)[:, None] == pivots[None, :], axis=1)
    trailing = jnp.where(row_in[:, None] | col_in[None, :], 0.0, current)
    factor = jnp.concatenate(factors, axis=1)
    return (trailing, factor)


def solution(mesh):
    return jax.shard_map(
        body,
        mesh=mesh,
        in_specs=(P("row", "col"), P("col", "row"), P("col"), P(), P(), P(), P(), P()),
        out_specs=(P("row", "col"), P("row", None)),
        check_vma=False,
    )
```

profile of v0, /device:TPU:0, one launch (start us, length us, event | category | flops | bytes accessed | tf_op | source)
XLA Modules:
  0.0 721.7 jit_solution(9475887452106300543)
XLA Ops:
  7.2 0.9 select_reduce_fusion.1
  9.2 7.3 %all-to-all-start.1 = ((s32[8,1,2]{2,1,0:T(1,128)}), s32[8,1,2]{2,1,0:T(1,128)S(1)}, u32[]{:S(2)}, u32[]{:S(2)}) async-start(s32[8,1,2]{2,1,0:T(1,128)} %copy.32), calls=%async_computation.1 | async-start | bytes 8192 | tf_op jit(solution)/shard_map/all_to_all | solution.py:63
  16.7 0.8 copy.31
  18.2 2.3 reduce-window.6
  21.3 1.6 gather_fusion
  22.9 6.0 all-to-all-start
  30.2 6.4 all-to-all-done
  36.8 18.0 %convolution_add_fusion = f32[3072,1536]{1,0:T(8,128)} fusion(f32[3072,1536]{1,0:T(8,128)} %param.10, f32[16,3072]{1,0:T(8,128)S(1)} %reshape.189, s32[16]{0:T(128)S(1)} %eq.152), kind=kOutput, calls=%fused_computation.7 | convolution fusion | flops 910712832 | bytes 37945408 | tf_op jit(solution)/shard_map/dot_general | solution.py:69
  54.8 18.7 %copy.33 = f32[3072,1536]{0,1:T(8,128)} copy(f32[3072,1536]{1,0:T(8,128)} %convolution_add_fusion) | data formatting | bytes 37748736 | tf_op jit(solution)/shard_map/add | solution.py:69
  73.4 8.2 %gather_fusion.1 = f32[128,3072]{1,0:T(8,128)S(1)} fusion(f32[3072,1536]{0,1:T(8,128)} %copy.33, s32[1024]{0:T(1024)S(1)} %pad_clamp_fusion), kind=kCustom, calls=%fused_computation.4 | custom fusion | bytes 3146240 | tf_op jit(solution)/shard_map/jit(_take)/gather | solution.py:29
  81.7 1.4 select_bitcast_fusion.1
  84.1 173.5 %all-gather.2.cloned.1.call-done = f32[3072,1024]{0,1:T(8,128)} async-done(((f32[3072,128]{0,1:T(8,128)}), f32[3072,1024]{0,1:T(8,128)}) %all-gather.2.cloned.1.call-update) | async-done | bytes 12582928 | tf_op jit(solution)/shard_map/all_gather | solution.py:86
  257.6 16.5 %gather_fusion.2 = f32[1024,3072]{1,0:T(8,128)} fusion(f32[3072,1024]{0,1:T(8,128)} %all-gather.2.cloned.1.call-done, s32[1024]{0:T(1024)S(1)} %broadcast_clamp_fusion), kind=kCustom, calls=%fused_computation.5 | custom fusion | bytes 25169920 | tf_op jit(solution)/shard_map/jit(_take)/gather | solution.py:87
  274.1 12.6 %copy.34 = f32[1024,3072]{0,1:T(8,128)} copy(f32[1024,3072]{1,0:T(8,128)} %gather_fusion.2) | data formatting | bytes 25165824 | tf_op jit(solution)/shard_map/jit(_take)/gather | solution.py:87
  286.7 12.4 %select_bitcast_fusion = f32[3072,1024]{1,0:T(8,128)} fusion(f32[1024,3072]{0,1:T(8,128)} %copy.34, pred[1024]{0:T(1024)(128)(4,1)S(1)} %compare_and_fusion.2), kind=kLoop, calls=%fused_computation.9 | loop fusion | flops 3145728 | bytes 25166848 | tf_op jit(solution)/shard_map/jit(_take)/select_n | solution.py:87
  299.1 4.8 fusion
  304.0 3.7 fusion.40
  307.7 2.3 copy.35
  310.0 5.3 gather_fusion.3
  315.4 1.3 select_select_fusion.2
  316.9 5.3 multiply_add_fusion.3
  322.3 1.7 dynamic-slice_select_fusion.3
  324.0 27.4 %all-reduce.14.cloned.1.call-done = f32[1024,256]{1,0:T(8,128)} async-done(((f32[1024,256]{1,0:T(8,128)}), f32[1024,256]{1,0:T(8,128)}) %all-reduce.14.cloned.1.call-update) | async-done | bytes 1048592 | tf_op jit(solution)/shard_map/psum | solution.py:117
  351.4 7.3 %convolution_subtract_fusion.5 = f32[3072,256]{1,0:T(8,128)S(1)} fusion(f32[3072,256]{0,1:T(8,128)S(1)} %multiply_add_fusion.3, f32[3072,1024]{1,0:T(8,128)} %select_bitcast_fusion, f32[1024,256]{1,0:T(8,128)} %all-reduce.14.cloned.1.call-done), kind=kOutput, calls=%fused_computation.17 | convolution fusion | flops 2416705536 | bytes 9699328 | tf_op jit(solution)/shard_map/dot_general | solution.py:93
  358.7 4.1 fusion.13
  362.8 1.6 copy-done.4
  364.4 3.3 fusion.39
  367.8 3.5 copy.36
  371.3 6.6 gather_fusion.4
  377.8 2.5 select_select_fusion.1
  380.7 7.0 multiply_add_fusion.2
  387.6 8.0 %convolution_subtract_fusion.4 = f32[3072,256]{1,0:T(8,128)} fusion(f32[3072,256]{0,1:T(8,128)S(1)} %multiply_add_fusion.3, f32[3072,1024]{1,0:T(8,128)} %select_bitcast_fusion, f32[1024,256]{1,0:T(8,128)S(1)} %copy-done.19), kind=kOutput, calls=%fused_computation.16 | convolution fusion | flops 2416705536 | bytes 9699328 | tf_op jit(solution)/shard_map/dot_general | solution.py:93
  395.6 1.6 dynamic-slice_select_fusion.2
  397.3 8.3 %convolution_subtract_fusion.2 = f32[3072,256]{1,0:T(8,128)} fusion(f32[3072,256]{0,1:T(8,128)S(1)} %multiply_add_fusion.3, f32[3072,1024]{1,0:T(8,128)} %select_bitcast_fusion, f32[1024,256]{1,0:T(8,128)S(1)} %copy-done.19), kind=kOutput, calls=%fused_computation.14 | convolution fusion | flops 2416705536 | bytes 9699328 | tf_op jit(solution)/shard_map/dot_general | solution.py:93
  405.5 11.8 %all-reduce.16.cloned.1.call-done = f32[1024,256]{1,0:T(8,128)} async-done(((f32[1024,256]{1,0:T(8,128)}), f32[1024,256]{1,0:T(8,128)}) %all-reduce.16.cloned.1.call-update) | async-done | bytes 1048592 | tf_op jit(solution)/shard_map/psum | solution.py:117
  417.3 8.3 %convolution_subtract_fusion.3 = f32[3072,256]{1,0:T(8,128)S(1)} fusion(f32[3072,256]{1,0:T(8,128)} %convolution_subtract_fusion.4, f32[3072,256]{0,1:T(8,128)} %multiply_add_fusion.2, f32[1024,256]{1,0:T(8,128)} %all-reduce.16.cloned.1.call-done), kind=kOutput, calls=%fused_computation.15 | convolution fusion | flops 2416705536 | bytes 9699328 | tf_op jit(solution)/shard_map/dot_general | solution.py:93
  425.7 4.1 fusion.11
  429.8 1.7 copy-done.2
  431.4 3.3 fusion.38
  434.7 3.5 copy.37
  438.2 6.6 gather_fusion.5
  444.8 2.6 select_select_fusion
  447.7 7.0 multiply_add_fusion.1
  454.7 1.6 dynamic-slice_select_fusion.1
  456.3 0.8 copy-done.8
  457.2 8.1 %convolution_subtract_fusion.1 = f32[3072,256]{1,0:T(8,128)} fusion(f32[3072,256]{1,0:T(8,128)S(1)} %copy-done.16, f32[3072,256]{0,1:T(8,128)S(1)} %copy-done.8, f32[1024,256]{1,0:T(8,128)} %all-reduce.16.cloned.1.call-done), kind=kOutput, calls=%fused_computation.13 | convolution fusion | flops 2416705536 | bytes 9699328 | tf_op jit(solution)/shard_map/dot_general | solution.py:93
  465.3 19.0 %all-reduce.18.cloned.1.call-done = f32[1024,256]{1,0:T(8,128)} async-done(((f32[1024,256]{1,0:T(8,128)}), f32[1024,256]{1,0:T(8,128)}) %all-reduce.18.cloned.1.call-update) | async-done | bytes 1048592 | tf_op jit(solution)/shard_map/psum | solution.py:117
  484.4 8.3 %convolution_subtract_fusion = f32[3072,256]{1,0:T(8,128)S(1)} fusion(f32[3072,256]{1,0:T(8,128)} %convolution_subtract_fusion.1, f32[3072,256]{0,1:T(8,128)} %multiply_add_fusion.1, f32[1024,256]{1,0:T(8,128)} %all-reduce.18.cloned.1.call-done), kind=kOutput, calls=%fused_computation.12 | convolution fusion | flops 2416705536 | bytes 9699328 | tf_op jit(solution)/shard_map/dot_general | solution.py:93
  492.7 4.3 fusion.9
  497.0 1.7 copy-done.12
  498.7 1.7 dynamic-slice_select_fusion
  500.4 1.0 compare_reduce_fusion.1
  501.4 2.0 compare_reduce_fusion
  503.4 3.9 fusion.37
  508.0 1.3 multiply_add_fusion
  509.4 1.6 copy-done.15
  511.0 1.0 copy-done.14
  512.0 5.4 pad_maximum_fusion
  517.4 12.6 %copy.38 = f32[3072,1024]{1,0:T(8,128)} copy(f32[3072,1024]{0,1:T(8,128)} %pad_maximum_fusion) | data formatting | bytes 25165824
  530.0 90.6 %all-reduce.20.cloned.1.call-done = (f32[1536,256]{0,1:T(8,128)}, f32[1536,256]{0,1:T(8,128)}, f32[1536,256]{0,1:T(8,128)}, f32[1536,256]{0,1:T(8,128)}) async-done(((f32[1536,256]{0,1:T(8,128)}, f32[1536,256]{0,1:T(8,128)}, f32[1536,256]{0,1:T(8,128)}, f32[1536,256]{0,1:T(8,128)}), (f32[1536,256]{0,1:T(8,128)}, f32[1536,256]{0,1:T(8,128)}, f32[1536,256]{0,1:T(8,128)}, ...) | async-done | bytes 6291472 | tf_op jit(solution)/shard_map/psum | solution.py:12
  620.6 19.9 %fusion.44 = f32[3072,1536]{1,0:T(8,128)} fusion(f32[3072,256]{0,1:T(8,128)} %multiply_add_fusion.1, f32[1536,256]{0,1:T(8,128)} %get-tuple-element.11), kind=kOutput, calls=%fused_computation.119 | convolution fusion | flops 14495514624 | bytes 23592960 | tf_op jit(solution)/shard_map/dot_general | solution.py:111
  640.5 18.5 %fusion.43 = f32[3072,1536]{1,0:T(8,128)} fusion(f32[3072,256]{0,1:T(8,128)S(1)} %copy-done.10, f32[1536,256]{0,1:T(8,128)S(1)} %copy-done.18), kind=kOutput, calls=%fused_computation.118 | convolution fusion | flops 14495514624 | bytes 23592960 | tf_op jit(solution)/shard_map/dot_general | solution.py:111
  659.0 17.9 %fusion.42 = f32[3072,1536]{1,0:T(8,128)} fusion(f32[3072,256]{0,1:T(8,128)S(1)} %multiply_add_fusion.3, f32[1536,256]{0,1:T(8,128)S(1)} %copy-done.17), kind=kOutput, calls=%fused_computation.117 | convolution fusion | flops 14495514624 | bytes 23592960 | tf_op jit(solution)/shard_map/dot_general | solution.py:111
  676.9 38.1 %subtract_select_fusion = f32[3072,1536]{1,0:T(8,128)} fusion(f32[3072,1536]{1,0:T(8,128)} %fusion.44, f32[3072,1536]{1,0:T(8,128)} %fusion.43, f32[3072,1536]{1,0:T(8,128)} %convolution_add_fusion, f32[3072,1536]{1,0:T(8,128)} %fusion.42, f32[3072,256]{0,1:T(8,128)} %copy-done.15, f32[1536,256]{0,1:T(8,128)} %get-tuple-element.14, ...), kind=kOutput, calls=%fused_computation.6 | convolution fusion | flops 14523826176 | bytes 99095040 | tf_op jit(solution)/shard_map/dot_general | solution.py:111
  (86 shorter events, 6.7 us)
Async XLA Ops:
  7.2 9.3 %copy-start = (f32[8,3072]{1,0:T(8,128)S(1)}, f32[8,3072]{1,0:T(8,128)}, u32[]{:S(2)}) copy-start(f32[8,3072]{1,0:T(8,128)} %param.11) | copy-start | bytes 294916
  9.2 13.7 %all-to-all-start.1 = ((s32[8,1,2]{2,1,0:T(1,128)}), s32[8,1,2]{2,1,0:T(1,128)S(1)}, u32[]{:S(2)}, u32[]{:S(2)}) async-start(s32[8,1,2]{2,1,0:T(1,128)} %copy.32), calls=%async_computation.1 | async-start | bytes 8192 | tf_op jit(solution)/shard_map/all_to_all | solution.py:63
  22.9 13.8 %all-to-all-start = ((f32[8,2,3072]{2,1,0:T(2,128)}), f32[8,2,3072]{2,1,0:T(2,128)S(1)}, u32[]{:S(2)}, u32[]{:S(2)}) async-start(f32[8,2,3072]{2,1,0:T(2,128)} %copy.31), calls=%async_computation | async-start | bytes 393216 | tf_op jit(solution)/shard_map/all_to_all | solution.py:62
  28.9 228.7 %all-gather.2.cloned.1.call-start = ((), (), s32[]{:S(2)}) async-start(), calls=%async_computation.2 | async-start | bytes 14155776 | tf_op jit(solution)/shard_map/all_gather | solution.py:86
  81.7 2.1 copy-start.20
  81.7 2.1 copy-start.21
  81.7 2.3 copy-start.11
  81.7 2.3 copy-start.22
  83.2 268.2 %all-reduce.14.cloned.1.call-start = ((), (), s32[]{:S(2)}) async-start(), calls=%async_computation.3 | async-start | bytes 2097152 | tf_op jit(solution)/shard_map/psum | solution.py:117
  304.0 3.7 copy-start.6
  316.7 100.6 %all-reduce.16.cloned.1.call-start = ((), (), s32[]{:S(2)}) async-start(), calls=%async_computation.4 | async-start | bytes 2097152 | tf_op jit(solution)/shard_map/psum | solution.py:117
  316.9 5.4 copy-start.7
  362.8 1.7 copy-start.4
  380.4 103.9 %all-reduce.18.cloned.1.call-start = ((), (), s32[]{:S(2)}) async-start(), calls=%async_computation.5 | async-start | bytes 2097152 | tf_op jit(solution)/shard_map/psum | solution.py:117
  380.7 7.0 copy-start.19
  387.6 8.0 %copy-start.5 = (f32[3072,256]{0,1:T(8,128)S(1)}, f32[3072,256]{0,1:T(8,128)}, u32[]{:S(2)}) copy-start(f32[3072,256]{0,1:T(8,128)} %copy-done.4) | copy-start | bytes 9437188
  429.7 1.7 copy-start.2
  447.5 173.2 %all-reduce.20.cloned.1.call-start = ((), (), s32[]{:S(2)}) async-start(), calls=%async_computation.6 | async-start | bytes 12582912 | tf_op jit(solution)/shard_map/psum | solution.py:12
  447.7 7.1 copy-start.3
  447.7 8.7 %copy-start.16 = (f32[3072,256]{1,0:T(8,128)S(1)}, f32[3072,256]{1,0:T(8,128)}, u32[]{:S(2)}) copy-start(f32[3072,256]{1,0:T(8,128)} %convolution_subtract_fusion.2) | copy-start | bytes 9437188
  454.7 2.5 copy-start.8
  497.0 1.7 copy-start.12
  503.4 4.6 copy-start.13
  508.0 3.0 copy-start.9
  508.0 4.0 copy-start.14
  509.3 1.7 copy-start.15
  620.6 19.9 %copy-start.10 = (f32[3072,256]{0,1:T(8,128)S(1)}, f32[3072,256]{0,1:T(8,128)}, u32[]{:S(2)}) copy-start(f32[3072,256]{0,1:T(8,128)} %multiply_add_fusion.2) | copy-start | bytes 9437188
  620.6 19.9 %copy-start.18 = (f32[1536,256]{0,1:T(8,128)S(1)}, f32[1536,256]{0,1:T(8,128)}, u32[]{:S(2)}) copy-start(f32[1536,256]{0,1:T(8,128)} %get-tuple-element.12) | copy-start | bytes 4718596
  640.5 18.5 %copy-start.17 = (f32[1536,256]{0,1:T(8,128)S(1)}, f32[1536,256]{0,1:T(8,128)}, u32[]{:S(2)}) copy-start(f32[1536,256]{0,1:T(8,128)} %get-tuple-element.13) | copy-start | bytes 4718596
  676.9 38.1 %copy-start.1 = (f32[8,3072]{1,0:T(8,128)S(1)}, f32[8,3072]{1,0:T(8,128)}, u32[]{:S(2)}) copy-start(f32[8,3072]{1,0:T(8,128)} %param.11) | copy-start | bytes 294916
Sparse Core Ops, SparseCore 0:
  83.3 174.2 all-gather.1
  316.8 34.4 all-reduce.13
  380.5 36.7 all-reduce.15
  447.6 36.7 all-reduce.17
  500.5 120.0 all-reduce.19
where the time goes:
time: 728 us; the launch traced here: 722 us
  waiting for transfers between devices  329 us (45%)
  matrix products  178 us (24%)
  local copies, waits for them, and re-layouts  124 us (17%)
  other arithmetic  61.7 us (8%)
  starting transfers between devices  14.6 us (2%)
  between operations  14.4 us (2%)
    all_gather x1, waiting for transfers between devices, body(): gathered = lax.all_gather(compact, 'col', axis=1, tiled=True)  174 us
    dot_general x4, matrix products, body(): lax.dot_general(finish_columns, col_scaled, (((1,), (1,)), ((), ())), pre...  94.3 us
    psum x1, waiting for transfers between devices, broadcast(): return lax.psum(block, axis)  90.6 us
    psum x3, waiting for transfers between devices, body(): pivot_rows = lax.psum(pivot_part, 'row')  58.2 us
    dot_general x6, matrix products, body(): lax.dot_general(cols_before, rows_before[offset:offset + panel_width], ((...  48.4 us
    gather x2, local copies, waits for them, and re-layouts, body(): every_panel = jnp.take(gathered, piv_owner * per_owner + piv_rank, axis=1)  29.1 us
    unnamed x47, local copies, waits for them, and re-layouts  21.9 us
    add x4, other arithmetic, pair_scale(): scaled * diag_part + shifted_next * coupled + shifted_prev * coupled_prev  20.7 us
  transfers between devices with their start and end apart: 7, of which 6 were waited for; matrix products, arithmetic and copies ran while one was open for 11% of the time, Pallas kernels for 0%

commit v1 on v0

--- a/solution.py
+++ b/solution.py
@@ -5,6 +5,15 @@
 
 CAP = 2
 precise = lax.Precision.HIGHEST
+
+
+def added_up(x, mesh_axis):
+    devices = lax.axis_size(mesh_axis)
+    result, hop = (x, 1)
+    while hop < devices:
+        result = result + lax.ppermute(result, mesh_axis, [(i, i ^ hop) for i in range(devices)])
+        hop = 2 * hop
+    return result
 
 
 def broadcast(block, axis, holder):
@@ -114,7 +123,7 @@
         factors.append(finish_columns)
         if panel_index + 1 < panel_count:
             pivot_part = select_rows(finish_scaled, pivots, row_start)
-            pivot_rows = lax.psum(pivot_part, "row")
+            pivot_rows = added_up(pivot_part, "row")
             previous.append((finish_columns, pivot_rows))
     row_ids = row_start + jnp.arange(rows_blk, dtype=jnp.int32)
     row_in = jnp.any(row_ids[:, None] == pivots[None, :], axis=1)

time: 728 us -> 714 us (0.981)
  other arithmetic: 61.7 us -> 52.1 us
  local copies, waits for them, and re-layouts: 124 us -> 115 us
    ppermute x0 -> x6, waiting for transfers between devices: none -> 64.3 us  [added_up(): lax.ppermute(result, mesh_axis, [(i, i ^ hop) for i in range(devices)])]
    psum x3 -> x0, waiting for transfers between devices: 58.2 us -> none  [body(): pivot_rows = lax.psum(pivot_part, 'row')]
    add x4, other arithmetic: 20.7 us -> 7.58 us  [pair_scale(): scaled * diag_part + shifted_next * coupled + shifted_prev * coupled_prev]
    slice x4, local copies, waits for them, and re-layouts: 14.2 us -> 6.67 us  [pair_scale(): shifted_next = jnp.concatenate([scaled[:, 1:], zero_col], axis=1)]
    dot_general x6, matrix products: 48.4 us -> 40.9 us  [body(): lax.dot_general(cols_before, rows_before[offset:offset + panel_width], ((...]
  transfers between devices with their start and end apart: 7 -> 10, of which waited for: 6 -> 7; matrix products, arithmetic and copies ran while one was open for 11% -> 8% of each run, Pallas kernels for 0% -> 0%
where the time goes in v1:
time: 714 us; the launch traced here: 707 us
  waiting for transfers between devices  333 us (47%)
  matrix products  173 us (24%)
  local copies, waits for them, and re-layouts  115 us (16%)
  other arithmetic  52.1 us (7%)
  starting transfers between devices  18.3 us (3%)
  between operations  15.1 us (2%)
    all_gather x1, waiting for transfers between devices, body(): gathered = lax.all_gather(compact, 'col', axis=1, tiled=True)  174 us
    dot_general x4, matrix products, body(): lax.dot_general(finish_columns, col_scaled, (((1,), (1,)), ((), ())), pre...  94.3 us
    psum x1, waiting for transfers between devices, broadcast(): return lax.psum(block, axis)  88.4 us
    ppermute x6, waiting for transfers between devices, added_up(): lax.ppermute(result, mesh_axis, [(i, i ^ hop) for i in range(devices)])  64.3 us
    dot_general x6, matrix products, body(): lax.dot_general(cols_before, rows_before[offset:offset + panel_width], ((...  40.9 us
    gather x2, local copies, waits for them, and re-layouts, body(): every_panel = jnp.take(gathered, piv_owner * per_owner + piv_rank, axis=1)  29.1 us
    gather x3, local copies, waits for them, and re-layouts, select_rows(): return jnp.where(inside[:, None], jnp.take(matrix, clipped, axis=0), 0.0)  20.2 us
    dot_general x4, matrix products, body(): jnp.dot(panel_cols, jnp.transpose(linv[panel_index]), precision=precise)  20 us
  transfers between devices with their start and end apart: 10, of which 7 were waited for; matrix products, arithmetic and copies ran while one was open for 8% of the time, Pallas kernels for 0%

profile of v1, /device:TPU:0, one launch (start us, length us, event | category | flops | bytes accessed | tf_op | source)
XLA Modules:
  0.0 706.9 jit_solution(11838608188345294501)
XLA Ops:
  7.2 0.9 select_reduce_fusion.1
  9.2 7.3 %all-to-all-start.1 = ((s32[8,1,2]{2,1,0:T(1,128)}), s32[8,1,2]{2,1,0:T(1,128)S(1)}, u32[]{:S(2)}, u32[]{:S(2)}) async-start(s32[8,1,2]{2,1,0:T(1,128)} %copy.32), calls=%async_computation.1 | async-start | bytes 8192 | tf_op jit(solution)/shard_map/all_to_all | solution.py:72
  16.7 0.8 copy.31
  18.2 2.3 reduce-window.6
  21.3 1.6 gather_fusion
  22.9 6.0 all-to-all-start
  30.2 6.4 all-to-all-done
  36.8 18.0 %convolution_add_fusion = f32[3072,1536]{1,0:T(8,128)} fusion(f32[3072,1536]{1,0:T(8,128)} %param.10, f32[16,3072]{1,0:T(8,128)S(1)} %reshape.189, s32[16]{0:T(128)S(1)} %eq.152), kind=kOutput, calls=%fused_computation.7 | convolution fusion | flops 910712832 | bytes 37945408 | tf_op jit(solution)/shard_map/dot_general | solution.py:78
  54.8 18.6 %copy.33 = f32[3072,1536]{0,1:T(8,128)} copy(f32[3072,1536]{1,0:T(8,128)} %convolution_add_fusion) | data formatting | bytes 37748736 | tf_op jit(solution)/shard_map/add | solution.py:78
  73.4 8.2 %gather_fusion.1 = f32[128,3072]{1,0:T(8,128)S(1)} fusion(f32[3072,1536]{0,1:T(8,128)} %copy.33, s32[1024]{0:T(1024)S(1)} %pad_clamp_fusion), kind=kCustom, calls=%fused_computation.4 | custom fusion | bytes 3146240 | tf_op jit(solution)/shard_map/jit(_take)/gather | solution.py:38
  81.6 1.4 select_bitcast_fusion.1
  83.4 174.1 %all-gather.2.cloned.1.call-done = f32[3072,1024]{0,1:T(8,128)} async-done(((f32[3072,128]{0,1:T(8,128)}), f32[3072,1024]{0,1:T(8,128)}) %all-gather.2.cloned.1.call-update) | async-done | bytes 12582928 | tf_op jit(solution)/shard_map/all_gather | solution.py:95
  257.5 16.5 %gather_fusion.2 = f32[1024,3072]{1,0:T(8,128)} fusion(f32[3072,1024]{0,1:T(8,128)} %all-gather.2.cloned.1.call-done, s32[1024]{0:T(1024)S(1)} %broadcast_clamp_fusion), kind=kCustom, calls=%fused_computation.5 | custom fusion | bytes 25169920 | tf_op jit(solution)/shard_map/jit(_take)/gather | solution.py:96
  274.1 12.6 %copy.34 = f32[1024,3072]{0,1:T(8,128)} copy(f32[1024,3072]{1,0:T(8,128)} %gather_fusion.2) | data formatting | bytes 25165824 | tf_op jit(solution)/shard_map/jit(_take)/gather | solution.py:96
  286.7 12.4 %select_bitcast_fusion = f32[3072,1024]{1,0:T(8,128)} fusion(f32[1024,3072]{0,1:T(8,128)} %copy.34, pred[1024]{0:T(1024)(128)(4,1)S(1)} %compare_and_fusion.2), kind=kLoop, calls=%fused_computation.9 | loop fusion | flops 3145728 | bytes 25166848 | tf_op jit(solution)/shard_map/jit(_take)/select_n | solution.py:96
  299.1 4.9 fusion.3
  303.9 2.6 copy.35
  306.6 7.0 gather_fusion.3
  313.5 2.5 select_select_fusion.2
  316.3 2.7 collective-permute-done
  319.1 1.9 fusion.71
  321.0 1.5 collective-permute-start.1
  323.2 3.3 multiply_add_fusion.3
  326.5 19.8 %collective-permute-done.1 = f32[1024,256]{1,0:T(8,128)S(1)} collective-permute-done((f32[1024,256]{1,0:T(8,128)S(1)}, f32[1024,256]{1,0:T(8,128)S(1)}, u32[]{:S(2)}, u32[]{:S(2)}) %collective-permute-start.1) | collective-permute-done | bytes 1048608 | tf_op jit(solution)/shard_map/ppermute | solution.py:14
  346.4 7.6 %convolution_subtract_fusion.2 = f32[3072,256]{1,0:T(8,128)S(1)} fusion(f32[3072,256]{0,1:T(8,128)S(1)} %multiply_add_fusion.3, f32[3072,1024]{1,0:T(8,128)} %select_bitcast_fusion, f32[1024,256]{1,0:T(8,128)S(1)} %add.184), kind=kOutput, calls=%fused_computation.17 | convolution fusion | flops 2416705536 | bytes 9699328 | tf_op jit(solution)/shard_map/dot_general | solution.py:102
  354.0 5.6 fusion.19
  359.6 3.6 copy.36
  363.2 6.7 gather_fusion.4
  369.9 1.7 select_select_fusion.1
  371.7 3.1 dynamic-slice_select_fusion.3
  376.4 1.5 collective-permute-start.3
  377.9 1.6 dynamic-slice_select_fusion.2
  379.5 1.5 multiply_add_fusion.2
  381.0 21.0 %collective-permute-done.3 = f32[1024,256]{1,0:T(8,128)S(1)} collective-permute-done((f32[1024,256]{1,0:T(8,128)S(1)}, f32[1024,256]{1,0:T(8,128)S(1)}, u32[]{:S(2)}, u32[]{:S(2)}) %collective-permute-start.3) | collective-permute-done | bytes 1048608 | tf_op jit(solution)/shard_map/ppermute | solution.py:14
  402.1 5.4 fusion.11
  407.5 7.5 %fusion.2 = f32[3072,256]{1,0:T(8,128)S(1)} fusion(f32[3072,256]{1,0:T(8,128)S(1)} %fusion.11, f32[3072,256]{0,1:T(8,128)S(1)} %multiply_add_fusion.3, f32[3072,1024]{1,0:T(8,128)} %select_bitcast_fusion, f32[1024,256]{1,0:T(8,128)} %copy-done.16), kind=kOutput, calls=%fused_computation.16 | convolution fusion | flops 2417491968 | bytes 12845056 | tf_op jit(solution)/shard_map/dot_general | solution.py:102
  415.0 5.5 fusion.17
  420.5 3.6 copy.37
  424.1 6.5 gather_fusion.5
  430.6 1.6 select_select_fusion
  432.3 7.3 %fusion.8 = f32[3072,256]{1,0:T(8,128)S(1)} fusion(f32[3072,256]{0,1:T(8,128)} %copy-done.5, f32[1024,256]{1,0:T(8,128)} %copy-done.17), kind=kOutput, calls=%fused_computation.38 | convolution fusion | flops 2415919104 | bytes 6553600 | tf_op jit(solution)/shard_map/dot_general | solution.py:102
  439.7 0.7 fusion.44
  441.2 1.5 collective-permute-start.5
  442.8 1.6 dynamic-slice_select_fusion.1
  444.4 1.5 multiply_add_fusion.1
  445.9 20.8 %collective-permute-done.5 = f32[1024,256]{1,0:T(8,128)S(1)} collective-permute-done((f32[1024,256]{1,0:T(8,128)S(1)}, f32[1024,256]{1,0:T(8,128)S(1)}, u32[]{:S(2)}, u32[]{:S(2)}) %collective-permute-start.5) | collective-permute-done | bytes 1048608 | tf_op jit(solution)/shard_map/ppermute | solution.py:14
  466.7 5.5 fusion.6
  472.3 7.5 %fusion.1 = f32[3072,256]{1,0:T(8,128)S(1)} fusion(f32[3072,256]{1,0:T(8,128)S(1)} %fusion.6, f32[3072,256]{1,0:T(8,128)S(1)} %fusion.8, f32[3072,256]{0,1:T(8,128)S(1)} %multiply_add_fusion.3, f32[3072,1024]{1,0:T(8,128)} %select_bitcast_fusion, f32[1024,256]{1,0:T(8,128)} %copy-done.16), kind=kOutput, calls=%fused_computation.14 | convolution fusion | flops 2418278400 | bytes 15990784 | tf_op jit(solution)/shard_map/dot_general | solution.py:102
  479.8 4.1 fusion.15
  483.9 1.7 copy-done.9
  485.6 1.6 dynamic-slice_select_fusion
  487.3 1.0 compare_reduce_fusion.1
  488.3 2.2 compare_reduce_fusion
  490.5 4.5 fusion.43
  495.1 1.3 multiply_add_fusion
  496.4 1.6 copy-done.13
  498.1 1.0 copy-done.12
  499.1 5.2 pad_maximum_fusion
  504.2 12.6 %copy.38 = f32[3072,1024]{1,0:T(8,128)} copy(f32[3072,1024]{0,1:T(8,128)} %pad_maximum_fusion) | data formatting | bytes 25165824
  516.9 88.4 %all-reduce.11.cloned.1.call-done = (f32[1536,256]{0,1:T(8,128)}, f32[1536,256]{0,1:T(8,128)}, f32[1536,256]{0,1:T(8,128)}, f32[1536,256]{0,1:T(8,128)}) async-done(((f32[1536,256]{0,1:T(8,128)}, f32[1536,256]{0,1:T(8,128)}, f32[1536,256]{0,1:T(8,128)}, f32[1536,256]{0,1:T(8,128)}), (f32[1536,256]{0,1:T(8,128)}, f32[1536,256]{0,1:T(8,128)}, f32[1536,256]{0,1:T(8,128)}, ...) | async-done | bytes 6291472 | tf_op jit(solution)/shard_map/psum | solution.py:21
  605.2 19.9 %fusion.50 = f32[3072,1536]{1,0:T(8,128)} fusion(f32[3072,256]{0,1:T(8,128)} %copy-done.11, f32[1536,256]{0,1:T(8,128)} %get-tuple-element.11), kind=kOutput, calls=%fused_computation.123 | convolution fusion | flops 14495514624 | bytes 23592960 | tf_op jit(solution)/shard_map/dot_general | solution.py:120
  625.1 18.3 %fusion.49 = f32[3072,1536]{1,0:T(8,128)} fusion(f32[3072,256]{0,1:T(8,128)S(1)} %copy-done.7, f32[1536,256]{0,1:T(8,128)S(1)} %copy-done.19), kind=kOutput, calls=%fused_computation.122 | convolution fusion | flops 14495514624 | bytes 23592960 | tf_op jit(solution)/shard_map/dot_general | solution.py:120
  643.4 17.9 %fusion.48 = f32[3072,1536]{1,0:T(8,128)} fusion(f32[3072,256]{0,1:T(8,128)S(1)} %multiply_add_fusion.3, f32[1536,256]{0,1:T(8,128)S(1)} %copy-done.18), kind=kOutput, calls=%fused_computation.121 | convolution fusion | flops 14495514624 | bytes 23592960 | tf_op jit(solution)/shard_map/dot_general | solution.py:120
  661.4 38.2 %subtract_select_fusion = f32[3072,1536]{1,0:T(8,128)} fusion(f32[3072,1536]{1,0:T(8,128)} %fusion.50, f32[3072,1536]{1,0:T(8,128)} %fusion.49, f32[3072,1536]{1,0:T(8,128)} %convolution_add_fusion, f32[3072,1536]{1,0:T(8,128)} %fusion.48, f32[3072,256]{0,1:T(8,128)} %copy-done.13, f32[1536,256]{0,1:T(8,128)} %get-tuple-element.14, ...), kind=kOutput, calls=%fused_computation.6 | convolution fusion | flops 14523826176 | bytes 99095040 | tf_op jit(solution)/shard_map/dot_general | solution.py:120
  (94 shorter events, 8.3 us)
Async XLA Ops:
  7.2 9.3 %copy-start = (f32[8,3072]{1,0:T(8,128)S(1)}, f32[8,3072]{1,0:T(8,128)}, u32[]{:S(2)}) copy-start(f32[8,3072]{1,0:T(8,128)} %param.11) | copy-start | bytes 294916
  9.2 13.7 %all-to-all-start.1 = ((s32[8,1,2]{2,1,0:T(1,128)}), s32[8,1,2]{2,1,0:T(1,128)S(1)}, u32[]{:S(2)}, u32[]{:S(2)}) async-start(s32[8,1,2]{2,1,0:T(1,128)} %copy.32), calls=%async_computation.1 | async-start | bytes 8192 | tf_op jit(solution)/shard_map/all_to_all | solution.py:72
  22.9 13.8 %all-to-all-start = ((f32[8,2,3072]{2,1,0:T(2,128)}), f32[8,2,3072]{2,1,0:T(2,128)S(1)}, u32[]{:S(2)}, u32[]{:S(2)}) async-start(f32[8,2,3072]{2,1,0:T(2,128)} %copy.31), calls=%async_computation | async-start | bytes 393216 | tf_op jit(solution)/shard_map/all_to_all | solution.py:71
  28.9 228.7 %all-gather.2.cloned.1.call-start = ((), (), s32[]{:S(2)}) async-start(), calls=%async_computation.2 | async-start | bytes 14155776 | tf_op jit(solution)/shard_map/all_gather | solution.py:95
  81.6 1.7 copy-start.8
  83.1 522.2 %all-reduce.11.cloned.1.call-start = ((), (), s32[]{:S(2)}) async-start(), calls=%async_computation.3 | async-start | bytes 12582912 | tf_op jit(solution)/shard_map/psum | solution.py:21
  303.9 18.6 %copy-start.2 = (f32[3072,256]{0,1:T(8,128)}, f32[3072,256]{0,1:T(8,128)S(1)}, u32[]{:S(2)}) copy-start(f32[3072,256]{0,1:T(8,128)S(1)} %fusion.3) | copy-start | bytes 9437188
  306.6 9.5 %copy-start.20 = (f32[1024]{0:T(1024)S(1)}, f32[1024]{0:T(1024)}, u32[]{:S(2)}) copy-start(f32[1024]{0:T(1024)} %param.17) | copy-start | bytes 12292
  306.6 9.5 %copy-start.21 = (s32[1024]{0:T(1024)S(1)}, s32[1024]{0:T(1024)}, u32[]{:S(2)}) copy-start(s32[1024]{0:T(1024)} %param.14) | copy-start | bytes 12292
  306.6 9.5 %copy-start.22 = (f32[1024]{0:T(1024)S(1)}, f32[1024]{0:T(1024)}, u32[]{:S(2)}) copy-start(f32[1024]{0:T(1024)} %param.16) | copy-start | bytes 12292
  316.1 3.0 collective-permute-start
  321.0 25.3 %collective-permute-start.1 = (f32[1024,256]{1,0:T(8,128)S(1)}, f32[1024,256]{1,0:T(8,128)S(1)}, u32[]{:S(2)}, u32[]{:S(2)}) collective-permute-start(f32[1024,256]{1,0:T(8,128)S(1)} %fusion.71), channel_id=1, source_target_pairs={{0,16},{8,24},{16,0},{24,8},{1,17},{9,25},{17,1},{25,9},{2,18},{10... | collective-permute-start | bytes 3145736 | tf_op jit(solution)/shard_map/ppermute | solution.py:14
  346.4 7.6 %copy-start.16 = (f32[1024,256]{1,0:T(8,128)}, f32[1024,256]{1,0:T(8,128)S(1)}, u32[]{:S(2)}) copy-start(f32[1024,256]{1,0:T(8,128)S(1)} %add.184) | copy-start | bytes 3145732
  369.9 4.9 copy-start.4
  371.6 3.9 collective-permute-start.2
  374.8 1.2 copy-start.15
  376.4 25.6 %collective-permute-start.3 = (f32[1024,256]{1,0:T(8,128)S(1)}, f32[1024,256]{1,0:T(8,128)S(1)}, u32[]{:S(2)}, u32[]{:S(2)}) collective-permute-start(f32[1024,256]{1,0:T(8,128)S(1)} %fusion.70), channel_id=1, source_target_pairs={{0,16},{8,24},{16,0},{24,8},{1,17},{9,25},{17,1},{25,9},{2,18},{10... | collective-permute-start | bytes 3145736 | tf_op jit(solution)/shard_map/ppermute | solution.py:14
  381.0 26.5 %copy-start.5 = (f32[3072,256]{0,1:T(8,128)}, f32[3072,256]{0,1:T(8,128)S(1)}, u32[]{:S(2)}) copy-start(f32[3072,256]{0,1:T(8,128)S(1)} %multiply_add_fusion.2) | copy-start | bytes 9437188
  402.1 5.4 copy-start.17
  432.2 7.4 %copy-start.3 = (f32[3072,256]{0,1:T(8,128)S(1)}, f32[3072,256]{0,1:T(8,128)}, u32[]{:S(2)}) copy-start(f32[3072,256]{0,1:T(8,128)} %fusion.17) | copy-start | bytes 9437188
  432.2 8.2 %collective-permute-start.4 = (f32[1024,256]{1,0:T(8,128)S(1)}, f32[1024,256]{1,0:T(8,128)S(1)}, u32[]{:S(2)}, u32[]{:S(2)}) collective-permute-start(f32[1024,256]{1,0:T(8,128)S(1)} %select_select_fusion), channel_id=1, source_target_pairs={{0,8},{8,0},{16,24},{24,16},{1,9},{9,1},{17,25},{25,17},{2,10},{10... | collective-permute-start | bytes 3145736 | tf_op jit(solution)/shard_map/ppermute | solution.py:14
  439.7 1.2 copy-start.14
  441.2 25.5 %collective-permute-start.5 = (f32[1024,256]{1,0:T(8,128)S(1)}, f32[1024,256]{1,0:T(8,128)S(1)}, u32[]{:S(2)}, u32[]{:S(2)}) collective-permute-start(f32[1024,256]{1,0:T(8,128)S(1)} %fusion.69), channel_id=1, source_target_pairs={{0,16},{8,24},{16,0},{24,8},{1,17},{9,25},{17,1},{25,9},{2,18},{10... | collective-permute-start | bytes 3145736 | tf_op jit(solution)/shard_map/ppermute | solution.py:14
  445.9 26.4 %copy-start.11 = (f32[3072,256]{0,1:T(8,128)}, f32[3072,256]{0,1:T(8,128)S(1)}, u32[]{:S(2)}) copy-start(f32[3072,256]{0,1:T(8,128)S(1)} %multiply_add_fusion.1) | copy-start | bytes 9437188
  483.9 1.7 copy-start.9
  490.5 4.5 copy-start.10
  495.1 3.0 copy-start.6
  495.1 4.0 copy-start.12
  496.4 1.7 copy-start.13
  605.2 19.9 %copy-start.7 = (f32[3072,256]{0,1:T(8,128)S(1)}, f32[3072,256]{0,1:T(8,128)}, u32[]{:S(2)}) copy-start(f32[3072,256]{0,1:T(8,128)} %copy-done.5) | copy-start | bytes 9437188
  605.2 19.9 %copy-start.19 = (f32[1536,256]{0,1:T(8,128)S(1)}, f32[1536,256]{0,1:T(8,128)}, u32[]{:S(2)}) copy-start(f32[1536,256]{0,1:T(8,128)} %get-tuple-element.12) | copy-start | bytes 4718596
  625.1 18.3 %copy-start.18 = (f32[1536,256]{0,1:T(8,128)S(1)}, f32[1536,256]{0,1:T(8,128)}, u32[]{:S(2)}) copy-start(f32[1536,256]{0,1:T(8,128)} %get-tuple-element.13) | copy-start | bytes 4718596
  661.4 38.2 %copy-start.1 = (f32[8,3072]{1,0:T(8,128)S(1)}, f32[8,3072]{1,0:T(8,128)}, u32[]{:S(2)}) copy-start(f32[8,3072]{1,0:T(8,128)} %param.11) | copy-start | bytes 294916
Sparse Core Ops, SparseCore 0:
  83.2 174.2 all-gather.1
  487.4 117.8 all-reduce.10
